TPU v7x, 256 devices: a whole 4x4x8 slice. The times are simulated.
256 devices in a mesh: row: 16 (over z_hi, x), col: 16 (over z_lo, y, core).
Axes of the slice: x: 4, y: 4, z: 8 (z_hi: 4, z_lo: 2; z = z_hi * 2 + z_lo), core: 2. Of those that a mesh axis runs over, the one named last changes fastest.
Arguments:
- signal: bfloat16 [32768, 2048], P('row', 'col'), may hold values from -40 to 40
- norm_gain: float32 [2048], replicated, may hold values from 0.5 to 2
- qkv_weight: bfloat16 [2048, 6144], P('row', 'col'), may hold values from -4 to 4
- out_weight: bfloat16 [2048, 2048], P('row', 'col'), may hold values from -1 to 1
Outputs:
- layer_out: bfloat16 [32768, 2048], P('row', 'col')
All inputs are finite; a program needn't handle non-finite values.
Results may differ from a plain program's by a relative error of at most 0.006.
Values may be sent and summed in bfloat16 or wider, within the bound.
No kernel may reach another device: no remote copies, remote signals or barrier semaphores. Data moves between devices by JAX's collectives and lax.ppermute only.
A program may use at most 64 MiB of HBM per device.

v0:
```python
import math
import jax
import jax.numpy as jnp
from jax import lax
from jax.sharding import PartitionSpec as P

HS = 128
COLS = 1024
EPSILON = 1e-05
NEGATIVE = -1e30


def row_softmax(row_block):
    head_size = row_block.shape[-1] // 3
    queries = row_block[..., :head_size]
    key_part = row_block[..., head_size : 2 * head_size]
    values = row_block[..., 2 * head_size :]
    factor = 1.0 / math.sqrt(head_size)
    scores = (
        jnp.einsum("chd,ehd->hce", queries, key_part, preferred_element_type=jnp.float32) * factor
    )
    length = row_block.shape[0]
    causal = jnp.arange(length)[:, None] >= jnp.arange(length)[None, :]
    scores = jnp.where(causal, scores, NEGATIVE)
    maxima = jnp.max(scores, axis=-1)
    weights = jnp.where(causal, jnp.exp(scores - maxima[..., None]), 0.0)
    totals = jnp.sum(weights, axis=-1)
    summed = jnp.einsum(
        "hce,ehd->chd", weights.astype(jnp.bfloat16), values, preferred_element_type=jnp.float32
    )
    return (summed, maxima.T, totals.T)


def column_softmax(gathered):
    head_size = gathered.shape[-1] // 3
    queries = gathered[..., :head_size]
    key_part = gathered[..., head_size : 2 * head_size]
    values = gathered[..., 2 * head_size :]
    factor = 1.0 / math.sqrt(head_size)
    scores = (
        jnp.einsum("rchd,schd->chrs", queries, key_part, preferred_element_type=jnp.float32)
        * factor
    )
    length = gathered.shape[0]
    earlier = jnp.arange(length)[:, None] > jnp.arange(length)[None, :]
    scores = jnp.where(earlier, scores, NEGATIVE)
    maxima = jnp.max(scores, axis=-1)
    weights = jnp.where(earlier, jnp.exp(scores - maxima[..., None]), 0.0)
    totals = jnp.sum(weights, axis=-1)
    summed = jnp.einsum(
        "chrs,schd->rchd", weights.astype(jnp.bfloat16), values, preferred_element_type=jnp.float32
    )
    maxima_rows = jnp.transpose(maxima, (2, 0, 1))
    totals_rows = jnp.transpose(totals, (2, 0, 1))
    return (
        lax.all_to_all(summed, "row", split_axis=0, concat_axis=1, tiled=True),
        lax.all_to_all(maxima_rows, "row", split_axis=0, concat_axis=1, tiled=True),
        lax.all_to_all(totals_rows, "row", split_axis=0, concat_axis=1, tiled=True),
    )


def per_device(signal, norm_gain, qkv_weight, out_weight):
    samples = signal.shape[0]
    gathered = lax.all_gather(signal, "col", axis=1, tiled=True)
    widened = gathered.astype(jnp.float32)
    average = jnp.mean(widened, axis=1, keepdims=True)
    variance = jnp.mean((widened - average) ** 2, axis=1, keepdims=True)
    normed = ((widened - average) * lax.rsqrt(variance + EPSILON) * norm_gain).astype(jnp.bfloat16)
    qkv_width = qkv_weight.shape[1]
    piece_qkv = lax.all_gather(qkv_weight, "row", axis=0, tiled=True)
    piece_out = lax.all_gather(out_weight, "row", axis=0, tiled=True)
    projected_sum = jnp.dot(normed, piece_qkv, preferred_element_type=jnp.float32)
    qkv = projected_sum.astype(jnp.bfloat16)
    rows_here = samples // COLS
    heads_here = qkv_width // (3 * HS)
    stacked = qkv.reshape(rows_here, COLS, heads_here, 3 * HS)
    row_acc, row_max, row_total = lax.map(row_softmax, stacked)
    col_acc, col_max, col_total = column_softmax(
        lax.all_to_all(stacked, "row", split_axis=1, concat_axis=0, tiled=True)
    )
    highest = jnp.maximum(row_max, col_max)
    row_factor = jnp.exp(row_max - highest)
    col_factor = jnp.exp(col_max - highest)
    denominator = row_factor * row_total + col_factor * col_total
    merged = (row_factor[..., None] * row_acc + col_factor[..., None] * col_acc) / denominator[
        ..., None
    ]
    attended = merged.astype(jnp.bfloat16).reshape(samples, heads_here * HS)
    residual = signal.astype(jnp.float32)
    branch = jnp.dot(
        lax.all_gather(attended, "col", axis=1, tiled=True),
        piece_out,
        preferred_element_type=jnp.float32,
    )
    return (residual + branch).astype(jnp.bfloat16)


def solution(mesh):
    return jax.shard_map(
        per_device,
        mesh=mesh,
        in_specs=(P("row", "col"), P(), P("row", "col"), P("row", "col")),
        out_specs=P("row", "col"),
        check_vma=False,
    )
```

profile of v0, /device:TPU:1, one launch (start us, length us, event | category | flops | bytes accessed | tf_op | source)
XLA Modules:
  0.0 338.2 jit_solution(2449595090421957147)
XLA Ops:
  8.0 69.0 %all-gather.4.cloned.1.call-done = bf16[2048,2048]{1,0:T(8,128)(2,1)} async-done(((bf16[2048,128]{1,0:T(8,128)(2,1)}), bf16[2048,2048]{1,0:T(8,128)(2,1)}) %all-gather.4.cloned.1.call-update) | async-done | bytes 8388624 | tf_op jit(solution)/shard_map/all_gather | solution.py:64
  77.0 4.7 %convert_reduce_fusion = f32[2048]{0:T(1024)S(1)} fusion(bf16[2048,2048]{1,0:T(8,128)(2,1)} %all-gather.4.cloned.1.call-done), kind=kLoop, calls=%fused_computation.18 | loop fusion | flops 8386560 | bytes 8396800 | tf_op jit(solution)/shard_map/reduce_sum | solution.py:66
  81.7 1.1 copy-done.1
  82.8 2.3 fusion.14
  85.1 47.5 %all-gather.6.cloned.1.call-done = bf16[2048,384]{1,0:T(8,128)(2,1)} async-done(((bf16[128,384]{1,0:T(8,128)(2,1)}), bf16[2048,384]{1,0:T(8,128)(2,1)}) %all-gather.6.cloned.1.call-update) | async-done | bytes 1572880 | tf_op jit(solution)/shard_map/all_gather | solution.py:70
  132.6 8.5 %fusion.22 = bf16[2048,384]{1,0:T(8,128)(2,1)S(1)} fusion(bf16[2048,384]{1,0:T(8,128)(2,1)} %all-gather.6.cloned.1.call-done, bf16[2048,2048]{1,0:T(8,128)(2,1)} %all-gather.4.cloned.1.call-done, f32[2048]{0:T(1024)S(1)} %copy-done.4, f32[2048]{0:T(1024)S(1)} %add_rsqrt_fusion, f32[2048]{0:T(1024)S(1)} %broadcast_multiply_fusion), kind=kOutput, calls=%fused_computation.28 | convolution fusion | flops 3242983424 | bytes 11558912 | tf_op jit(solution)/shard_map/dot_general | solution.py:72
  141.1 2.8 copy.55
  143.9 5.8 %all-to-all-start = ((bf16[2,1024,1,384]{3,0,2,1:T(2,128)(2,1)}), bf16[2,1024,1,384]{3,0,2,1:T(2,128)(2,1)}, u32[]{:S(2)}, u32[]{:S(2)}) async-start(bf16[2,1024,1,384]{3,0,2,1:T(2,128)(2,1)} %copy.55), calls=%async_computation | async-start | bytes 3145728 | tf_op jit(solution)/shard_map/all_to_all | solution.py:79
  149.7 27.8 %all-to-all-done = bf16[2,1024,1,384]{3,0,2,1:T(2,128)(2,1)} async-done(((bf16[2,1024,1,384]{3,0,2,1:T(2,128)(2,1)}), bf16[2,1024,1,384]{3,0,2,1:T(2,128)(2,1)}, u32[]{:S(2)}, u32[]{:S(2)}) %all-to-all-start) | async-done | bytes 1572896 | tf_op jit(solution)/shard_map/all_to_all | solution.py:79
  177.4 2.5 copy.84
  179.9 1.5 all_to_all.55
  181.5 1.6 fusion.29
  183.1 0.8 copy.57
  186.5 7.8 %all-to-all-start.3 = ((f32[16,1,128]{2,1,0:T(1,128)}), f32[16,1,128]{2,1,0:T(1,128)S(1)}, u32[]{:S(2)}, u32[]{:S(2)}) async-start(f32[16,1,128]{2,1,0:T(1,128)} %reshape.99), calls=%async_computation.3 | async-start | bytes 16384 | tf_op jit(solution)/shard_map/all_to_all | solution.py:58
  196.8 6.5 %all-to-all-done.3 = f32[16,1,128]{2,1,0:T(1,128)S(1)} async-done(((f32[16,1,128]{2,1,0:T(1,128)}), f32[16,1,128]{2,1,0:T(1,128)S(1)}, u32[]{:S(2)}, u32[]{:S(2)}) %all-to-all-start.3) | async-done | bytes 8224 | tf_op jit(solution)/shard_map/all_to_all | solution.py:58
  203.2 3.5 %all-to-all-start.1 = ((f32[16,1,128]{2,1,0:T(1,128)}), f32[16,1,128]{2,1,0:T(1,128)S(1)}, u32[]{:S(2)}, u32[]{:S(2)}) async-start(f32[16,1,128]{2,1,0:T(1,128)} %reshape.101), calls=%async_computation.1 | async-start | bytes 16384 | tf_op jit(solution)/shard_map/all_to_all | solution.py:57
  206.7 1.3 convolution_bitcast_fusion
  208.0 1.6 copy.66
  209.7 5.8 %all-to-all-done.1 = f32[16,1,128]{2,1,0:T(1,128)S(1)} async-done(((f32[16,1,128]{2,1,0:T(1,128)}), f32[16,1,128]{2,1,0:T(1,128)S(1)}, u32[]{:S(2)}, u32[]{:S(2)}) %all-to-all-start.1) | async-done | bytes 8224 | tf_op jit(solution)/shard_map/all_to_all | solution.py:57
  215.4 4.4 %all-to-all-start.2 = ((f32[32,64,1,128]{3,1,2,0:T(8,128)}), f32[32,64,1,128]{3,1,2,0:T(8,128)}, u32[]{:S(2)}, u32[]{:S(2)}) async-start(f32[32,64,1,128]{3,1,2,0:T(8,128)} %copy.66), calls=%async_computation.2 | async-start | bytes 2097152 | tf_op jit(solution)/shard_map/all_to_all | solution.py:56
  219.8 14.5 %while.14 = (s32[]{:T(128)}, f32[2,1024,1,128]{3,1,0,2:T(8,128)}, f32[2,1024,1]{1,0,2:T(2,128)S(1)}, f32[2,1024,1]{1,0,2:T(2,128)S(1)}, bf16[2,1024,1,384]{3,1,2,0:T(8,128)(2,1)S(1)}, /*index=5*/s32[]{:T(128)}, s32[]{:T(128)}) while((s32[]{:T(128)}, f32[2,1024,1,128]{3,1,0,2:T(8,128)}, f32[2,1024,1]{1,0,2:T(2,128)S(1)}, ...), condition=%wide.region_5.6_spmd, body=%wide.region_2.5_spmd.sunk | while | flops 553646080 | bytes 34374260 | solution.py:77
  220.7 1.9 copy-done
  223.5 0.8 constant_dynamic-update-slice_fusion.2
  224.3 2.7 fusion.48
  227.9 1.9 copy-done
  230.7 0.9 constant_dynamic-update-slice_fusion.2
  231.6 2.7 fusion.48
  236.3 1.3 copy.67
  237.6 2.8 fusion.28
  240.4 43.8 %all_gather.15 = bf16[2048,128]{1,0:T(8,128)(2,1)S(1)} all-gather(bf16[128,128]{1,0:T(8,128)(2,1)S(1)} %copy-done.3), channel_id=1, replica_groups=mesh['row'=16,'col'=16] {'row'}, dimensions={0}, use_global_device_ids=true | all-gather | bytes 557056 | tf_op jit(solution)/shard_map/all_gather | solution.py:71
  284.1 41.0 %all-gather.8.cloned.1.call-done = bf16[2048,2048]{1,0:T(8,128)(2,1)} async-done(((bf16[2048,128]{1,0:T(8,128)(2,1)}), bf16[2048,2048]{1,0:T(8,128)(2,1)}) %all-gather.8.cloned.1.call-update) | async-done | bytes 8388624 | tf_op jit(solution)/shard_map/all_gather | solution.py:91
  325.1 6.5 %fusion.25 = bf16[2048,128]{1,0:T(8,128)(2,1)} fusion(bf16[2048,2048]{1,0:T(8,128)(2,1)} %all-gather.8.cloned.1.call-done, bf16[2048,128]{1,0:T(8,128)(2,1)S(1)} %all_gather.15, bf16[2048,128]{1,0:T(8,128)(2,1)S(1)} %copy-done.2), kind=kOutput, calls=%fused_computation.30 | convolution fusion | flops 1074528256 | bytes 9961472 | tf_op jit(solution)/shard_map/dot_general | solution.py:90
  (55 shorter events, 11.9 us)
Async XLA Ops:
  6.5 70.5 %all-gather.4.cloned.1.call-start = ((), (), s32[]{:S(2)}) async-start(), calls=%async_computation.4 | async-start | bytes 8912896 | tf_op jit(solution)/shard_map/all_gather | solution.py:64
  7.3 125.4 %all-gather.6.cloned.1.call-start = ((), (), s32[]{:S(2)}) async-start(), calls=%async_computation.5 | async-start | bytes 1671168 | tf_op jit(solution)/shard_map/all_gather | solution.py:70
  77.0 5.8 %copy-start.1 = (bf16[2048,2048]{1,0:T(8,128)(2,1)S(1)}, bf16[2048,2048]{1,0:T(8,128)(2,1)}, u32[]{:S(2)}) copy-start(bf16[2048,2048]{1,0:T(8,128)(2,1)} %all-gather.4.cloned.1.call-done) | copy-start | bytes 25165828
  82.8 49.9 %copy-start.4 = (f32[2048]{0:T(1024)S(1)}, f32[2048]{0:T(1024)}, u32[]{:S(2)}) copy-start(f32[2048]{0:T(1024)} %param.7) | copy-start | bytes 24580
  143.9 33.6 %all-to-all-start = ((bf16[2,1024,1,384]{3,0,2,1:T(2,128)(2,1)}), bf16[2,1024,1,384]{3,0,2,1:T(2,128)(2,1)}, u32[]{:S(2)}, u32[]{:S(2)}) async-start(bf16[2,1024,1,384]{3,0,2,1:T(2,128)(2,1)} %copy.55), calls=%async_computation | async-start | bytes 3145728 | tf_op jit(solution)/shard_map/all_to_all | solution.py:79
  186.5 16.7 %all-to-all-start.3 = ((f32[16,1,128]{2,1,0:T(1,128)}), f32[16,1,128]{2,1,0:T(1,128)S(1)}, u32[]{:S(2)}, u32[]{:S(2)}) async-start(f32[16,1,128]{2,1,0:T(1,128)} %reshape.99), calls=%async_computation.3 | async-start | bytes 16384 | tf_op jit(solution)/shard_map/all_to_all | solution.py:58
  203.2 12.2 %all-to-all-start.1 = ((f32[16,1,128]{2,1,0:T(1,128)}), f32[16,1,128]{2,1,0:T(1,128)S(1)}, u32[]{:S(2)}, u32[]{:S(2)}) async-start(f32[16,1,128]{2,1,0:T(1,128)} %reshape.101), calls=%async_computation.1 | async-start | bytes 16384 | tf_op jit(solution)/shard_map/all_to_all | solution.py:57
  215.4 20.8 %all-to-all-start.2 = ((f32[32,64,1,128]{3,1,2,0:T(8,128)}), f32[32,64,1,128]{3,1,2,0:T(8,128)}, u32[]{:S(2)}, u32[]{:S(2)}) async-start(f32[32,64,1,128]{3,1,2,0:T(8,128)} %copy.66), calls=%async_computation.2 | async-start | bytes 2097152 | tf_op jit(solution)/shard_map/all_to_all | solution.py:56
  219.8 105.3 %all-gather.8.cloned.1.call-start = ((), (), s32[]{:S(2)}) async-start(), calls=%async_computation.6 | async-start | bytes 8912896 | tf_op jit(solution)/shard_map/all_gather | solution.py:91
  220.7 1.9 copy-start
  227.9 1.9 copy-start
  234.4 6.0 %copy-start.3 = (bf16[128,128]{1,0:T(8,128)(2,1)S(1)}, bf16[128,128]{1,0:T(8,128)(2,1)}, u32[]{:S(2)}) copy-start(bf16[128,128]{1,0:T(8,128)(2,1)} %param.9) | copy-start | bytes 98308
  234.4 90.7 %copy-start.2 = (bf16[2048,128]{1,0:T(8,128)(2,1)S(1)}, bf16[2048,128]{1,0:T(8,128)(2,1)}, u32[]{:S(2)}) copy-start(bf16[2048,128]{1,0:T(8,128)(2,1)} %param.6) | copy-start | bytes 1572868
Sparse Core Ops, SparseCore 0:
  9.1 67.8 all-gather.3
  79.4 53.1 all-gather.5
  240.5 84.5 all-gather.7
where the time goes:
time: 339 us; the launch traced here: 338 us
  waiting for transfers between devices  199 us (59%)
  blocking collectives  43.8 us (13%)
  starting transfers between devices  21.5 us (6%)
  local copies, waits for them, and re-layouts  21.3 us (6%)
  matrix products  20.6 us (6%)
  other arithmetic  18.6 us (5%)
  between operations  13.3 us (4%)
    all_gather x1, waiting for transfers between devices, per_device(): gathered = lax.all_gather(signal, 'col', axis=1, tiled=True)  69 us
    all_gather x1, waiting for transfers between devices, per_device(): piece_qkv = lax.all_gather(qkv_weight, 'row', axis=0, tiled=True)  47.5 us
    all_gather x1, blocking collectives, per_device(): piece_out = lax.all_gather(out_weight, 'row', axis=0, tiled=True)  43.8 us
    all_gather x1, waiting for transfers between devices, per_device(): lax.all_gather(attended, 'col', axis=1, tiled=True)  41 us
    all_to_all x1, waiting for transfers between devices, per_device(): lax.all_to_all(stacked, 'row', split_axis=1, concat_axis=0, tiled=True)  27.8 us
    dot_general x1, matrix products, per_device(): jnp.dot(normed, piece_qkv, preferred_element_type=jnp.float32)  8.46 us
    all_to_all x1, starting transfers between devices, column_softmax(): lax.all_to_all(totals_rows, 'row', split_axis=0, concat_axis=1, tiled=True)  7.84 us
  transfers between devices with their start and end apart: 7, of which 6 were waited for; matrix products, arithmetic and copies ran while one was open for 7% of the time, Pallas kernels for 0%

commit v1 on v0

--- a/solution.py
+++ b/solution.py
@@ -61,7 +61,9 @@
 
 def per_device(signal, norm_gain, qkv_weight, out_weight):
     samples = signal.shape[0]
-    gathered = lax.all_gather(signal, "col", axis=1, tiled=True)
+    gathered = jnp.concatenate(
+        lax.all_to_all(jnp.stack([signal] * lax.axis_size("col")), "col", 0, 0), axis=1
+    )
     widened = gathered.astype(jnp.float32)
     average = jnp.mean(widened, axis=1, keepdims=True)
     variance = jnp.mean((widened - average) ** 2, axis=1, keepdims=True)

time: 339 us -> 393 us (1.16)
  waiting for transfers between devices: 199 us -> 220 us
  starting transfers between devices: 21.5 us -> 37.3 us
  other arithmetic: 18.6 us -> 33.1 us
  local copies, waits for them, and re-layouts: 21.3 us -> 30.4 us
  blocking collectives: 43.8 us -> 37.8 us
    all_to_all x0 -> x1, waiting for transfers between devices: none -> 123 us  [per_device(): lax.all_to_all(jnp.stack([signal] * lax.axis_size('col')), 'col', 0, 0)]
    all_gather x1 -> x0, waiting for transfers between devices: 69 us -> none  [per_device(): gathered = lax.all_gather(signal, 'col', axis=1, tiled=True)]
    all_gather x1, waiting for transfers between devices: 47.5 us -> 0.01 us  [per_device(): piece_qkv = lax.all_gather(qkv_weight, 'row', axis=0, tiled=True)]
    all_to_all x1, waiting for transfers between devices: 27.8 us -> 39.6 us  [per_device(): lax.all_to_all(stacked, 'row', split_axis=1, concat_axis=0, tiled=True)]
    all_to_all x1, starting transfers between devices: 5.78 us -> 15.6 us  [per_device(): lax.all_to_all(stacked, 'row', split_axis=1, concat_axis=0, tiled=True)]
    convert_element_type x0 -> x1, other arithmetic: none -> 9.07 us  [per_device(): ((widened - average) * lax.rsqrt(variance + EPSILON) * norm_gain).astype(...]
    all_to_all x0 -> x1, starting transfers between devices: none -> 7.67 us  [per_device(): lax.all_to_all(jnp.stack([signal] * lax.axis_size('col')), 'col', 0, 0)]
    all_gather x1, blocking collectives: 43.8 us -> 37.8 us  [per_device(): piece_out = lax.all_gather(out_weight, 'row', axis=0, tiled=True)]
  transfers between devices with their start and end apart: 7 -> 7, of which waited for: 6 -> 6; matrix products, arithmetic and copies ran while one was open for 7% -> 10% of each run, Pallas kernels for 0% -> 0%
where the time goes in v1:
time: 393 us; the launch traced here: 392 us
  waiting for transfers between devices  220 us (56%)
  blocking collectives  37.8 us (10%)
  starting transfers between devices  37.3 us (9%)
  other arithmetic  33.1 us (8%)
  local copies, waits for them, and re-layouts  30.4 us (8%)
  matrix products  20.4 us (5%)
  between operations  13.6 us (3%)
    all_to_all x1, waiting for transfers between devices, per_device(): lax.all_to_all(jnp.stack([signal] * lax.axis_size('col')), 'col', 0, 0)  123 us
    all_gather x1, waiting for transfers between devices, per_device(): lax.all_gather(attended, 'col', axis=1, tiled=True)  41 us
    all_to_all x1, waiting for transfers between devices, per_device(): lax.all_to_all(stacked, 'row', split_axis=1, concat_axis=0, tiled=True)  39.6 us
    all_gather x1, blocking collectives, per_device(): piece_out = lax.all_gather(out_weight, 'row', axis=0, tiled=True)  37.8 us
    all_to_all x1, starting transfers between devices, per_device(): lax.all_to_all(stacked, 'row', split_axis=1, concat_axis=0, tiled=True)  15.6 us
    convert_element_type x1, other arithmetic, per_device(): ((widened - average) * lax.rsqrt(variance + EPSILON) * norm_gain).astype(...  9.07 us
    dot_general x1, matrix products, per_device(): jnp.dot(normed, piece_qkv, preferred_element_type=jnp.float32)  8.36 us
  transfers between devices with their start and end apart: 7, of which 6 were waited for; matrix products, arithmetic and copies ran while one was open for 10% of the time, Pallas kernels for 0%

profile of v1, /device:TPU:1, one launch (start us, length us, event | category | flops | bytes accessed | tf_op | source)
XLA Modules:
  0.0 392.3 jit_solution(18243611229706872594)
XLA Ops:
  7.8 4.3 %stack.2 = bf16[16,2048,128]{1,2,0:T(8,128)(2,1)} broadcast(bf16[2048,128]{0,1:T(8,128)(2,1)S(1)} %copy.58), dimensions={1,2} | broadcast | bytes 8912896 | tf_op jit(solution)/shard_map/stack | solution.py:65
  12.1 7.7 %all-to-all-start = ((bf16[16,2048,128]{1,2,0:T(8,128)(2,1)}), bf16[16,2048,128]{1,2,0:T(8,128)(2,1)}, u32[]{:S(2)}, u32[]{:S(2)}) async-start(bf16[16,2048,128]{1,2,0:T(8,128)(2,1)} %stack.2), calls=%async_computation | async-start | bytes 16777216 | tf_op jit(solution)/shard_map/all_to_all | solution.py:65
  20.5 122.6 %all-to-all-done = bf16[16,2048,128]{1,2,0:T(8,128)(2,1)} async-done(((bf16[16,2048,128]{1,2,0:T(8,128)(2,1)}), bf16[16,2048,128]{1,2,0:T(8,128)(2,1)}, u32[]{:S(2)}, u32[]{:S(2)}) %all-to-all-start) | async-done | bytes 8388640 | tf_op jit(solution)/shard_map/all_to_all | solution.py:65
  143.1 4.7 %convert_reduce_fusion = f32[2048]{0:T(1024)S(1)} fusion(bf16[16,2048,128]{1,2,0:T(8,128)(2,1)} %all-to-all-done), kind=kLoop, calls=%fused_computation.22 | loop fusion | flops 8386560 | bytes 8396800 | tf_op jit(solution)/shard_map/reduce_sum | solution.py:68
  147.8 5.6 %multiply_reduce_fusion = f32[2048]{0:T(1024)S(1)} fusion(bf16[16,2048,128]{1,2,0:T(8,128)(2,1)} %all-to-all-done, f32[2048]{0:T(1024)S(1)} %broadcast_multiply_fusion), kind=kLoop, calls=%fused_computation.21 | loop fusion | flops 16775168 | bytes 8404992 | tf_op jit(solution)/shard_map/reduce_sum | solution.py:69
  153.4 9.1 %fusion.14 = bf16[2048,2048]{0,1:T(8,128)(2,1)} fusion(bf16[16,2048,128]{1,2,0:T(8,128)(2,1)} %all-to-all-done, f32[2048]{0:T(1024)S(1)} %copy-done.3, f32[2048]{0:T(1024)S(1)} %add_rsqrt_fusion, f32[2048]{0:T(1024)S(1)} %broadcast_multiply_fusion), kind=kLoop, calls=%fused_computation.20 | loop fusion | flops 20971520 | bytes 16801792 | tf_op jit(solution)/shard_map/convert_element_type | solution.py:70
  162.5 8.4 %convolution_convert_fusion = bf16[2048,384]{1,0:T(8,128)(2,1)S(1)} fusion(bf16[2048,2048]{0,1:T(8,128)(2,1)} %fusion.14, bf16[2048,384]{1,0:T(8,128)(2,1)} %all-gather.3.cloned.1.call-done), kind=kOutput, calls=%fused_computation.23 | convolution fusion | flops 3222011904 | bytes 11534336 | tf_op jit(solution)/shard_map/dot_general | solution.py:74
  170.9 3.0 copy.60
  173.8 15.6 %all-to-all-start.1 = ((bf16[2,1024,1,384]{3,0,2,1:T(2,128)(2,1)}), bf16[2,1024,1,384]{3,0,2,1:T(2,128)(2,1)S(1)}, u32[]{:S(2)}, u32[]{:S(2)}) async-start(bf16[2,1024,1,384]{3,0,2,1:T(2,128)(2,1)} %copy.60), calls=%async_computation.1 | async-start | bytes 3145728 | tf_op jit(solution)/shard_map/all_to_all | solution.py:81
  189.5 39.6 %all-to-all-done.1 = bf16[2,1024,1,384]{3,0,2,1:T(2,128)(2,1)S(1)} async-done(((bf16[2,1024,1,384]{3,0,2,1:T(2,128)(2,1)}), bf16[2,1024,1,384]{3,0,2,1:T(2,128)(2,1)S(1)}, u32[]{:S(2)}, u32[]{:S(2)}) %all-to-all-start.1) | async-done | bytes 1572896 | tf_op jit(solution)/shard_map/all_to_all | solution.py:81
  229.1 2.2 copy.89
  231.4 3.7 all_to_all.59
  235.0 1.4 fusion.19
  236.4 2.7 copy.62
  240.4 1.3 fusion.21
  243.9 6.2 %all-to-all-start.4 = ((f32[16,1,128]{2,1,0:T(1,128)}), f32[16,1,128]{2,1,0:T(1,128)S(1)}, u32[]{:S(2)}, u32[]{:S(2)}) async-start(f32[16,1,128]{2,1,0:T(1,128)} %reshape.111), calls=%async_computation.4 | async-start | bytes 16384 | tf_op jit(solution)/shard_map/all_to_all | solution.py:58
  251.7 1.5 copy.70
  253.2 5.7 %all-to-all-done.4 = f32[16,1,128]{2,1,0:T(1,128)S(1)} async-done(((f32[16,1,128]{2,1,0:T(1,128)}), f32[16,1,128]{2,1,0:T(1,128)S(1)}, u32[]{:S(2)}, u32[]{:S(2)}) %all-to-all-start.4) | async-done | bytes 8224 | tf_op jit(solution)/shard_map/all_to_all | solution.py:58
  258.9 3.4 all-to-all-start.2
  263.7 1.6 copy.71
  265.3 5.9 %all-to-all-done.2 = f32[16,1,128]{2,1,0:T(1,128)S(1)} async-done(((f32[16,1,128]{2,1,0:T(1,128)}), f32[16,1,128]{2,1,0:T(1,128)S(1)}, u32[]{:S(2)}, u32[]{:S(2)}) %all-to-all-start.2) | async-done | bytes 8224 | tf_op jit(solution)/shard_map/all_to_all | solution.py:57
  271.1 4.3 %all-to-all-start.3 = ((f32[32,64,1,128]{3,1,2,0:T(8,128)}), f32[32,64,1,128]{3,1,2,0:T(8,128)}, u32[]{:S(2)}, u32[]{:S(2)}) async-start(f32[32,64,1,128]{3,1,2,0:T(8,128)} %copy.71), calls=%async_computation.3 | async-start | bytes 2097152 | tf_op jit(solution)/shard_map/all_to_all | solution.py:56
  275.5 14.5 %while.14 = (s32[]{:T(128)}, f32[2,1024,1,128]{3,1,0,2:T(8,128)}, f32[2,1024,1]{1,0,2:T(2,128)S(1)}, f32[2,1024,1]{1,0,2:T(2,128)S(1)}, bf16[2,1024,1,384]{3,1,2,0:T(8,128)(2,1)S(1)}, /*index=5*/s32[]{:T(128)}, s32[]{:T(128)}) while((s32[]{:T(128)}, f32[2,1024,1,128]{3,1,0,2:T(8,128)}, f32[2,1024,1]{1,0,2:T(2,128)S(1)}, ...), condition=%wide.region_5.6_spmd, body=%wide.region_2.5_spmd.sunk | while | flops 553646080 | bytes 34374260 | solution.py:79
  276.4 1.9 copy-done
  280.0 2.7 fusion.39
  283.6 1.9 copy-done
  287.3 2.7 fusion.39
  292.0 4.0 %all-to-all-done.3 = f32[32,64,1,128]{3,1,2,0:T(8,128)} async-done(((f32[32,64,1,128]{3,1,2,0:T(8,128)}), f32[32,64,1,128]{3,1,2,0:T(8,128)}, u32[]{:S(2)}, u32[]{:S(2)}) %all-to-all-start.3) | async-done | bytes 1048608 | tf_op jit(solution)/shard_map/all_to_all | solution.py:56
  297.3 2.8 fusion.18
  300.1 37.8 %all_gather.11 = bf16[2048,128]{1,0:T(8,128)(2,1)S(1)} all-gather(bf16[128,128]{1,0:T(8,128)(2,1)S(1)} %copy-done.2), channel_id=1, replica_groups=mesh['row'=16,'col'=16] {'row'}, dimensions={0}, use_global_device_ids=true | all-gather | bytes 557056 | tf_op jit(solution)/shard_map/all_gather | solution.py:73
  337.9 41.0 %all-gather.5.cloned.1.call-done = bf16[2048,2048]{1,0:T(8,128)(2,1)} async-done(((bf16[2048,128]{1,0:T(8,128)(2,1)}), bf16[2048,2048]{1,0:T(8,128)(2,1)}) %all-gather.5.cloned.1.call-update) | async-done | bytes 8388624 | tf_op jit(solution)/shard_map/all_gather | solution.py:93
  378.9 6.5 %fusion.15 = bf16[2048,128]{1,0:T(8,128)(2,1)} fusion(bf16[2048,2048]{1,0:T(8,128)(2,1)} %all-gather.5.cloned.1.call-done, bf16[2048,128]{1,0:T(8,128)(2,1)S(1)} %all_gather.11, bf16[2048,128]{1,0:T(8,128)(2,1)S(1)} %copy-done.1), kind=kOutput, calls=%fused_computation.25 | convolution fusion | flops 1074528256 | bytes 9961472 | tf_op jit(solution)/shard_map/dot_general | solution.py:92
  (55 shorter events, 16.8 us)
Async XLA Ops:
  12.1 131.0 %all-to-all-start = ((bf16[16,2048,128]{1,2,0:T(8,128)(2,1)}), bf16[16,2048,128]{1,2,0:T(8,128)(2,1)}, u32[]{:S(2)}, u32[]{:S(2)}) async-start(bf16[16,2048,128]{1,2,0:T(8,128)(2,1)} %stack.2), calls=%async_computation | async-start | bytes 16777216 | tf_op jit(solution)/shard_map/all_to_all | solution.py:65
  19.7 142.8 %all-gather.3.cloned.1.call-start = ((), (), s32[]{:S(2)}) async-start(), calls=%async_computation.5 | async-start | bytes 1671168 | tf_op jit(solution)/shard_map/all_gather | solution.py:72
  147.8 5.6 %copy-start.3 = (f32[2048]{0:T(1024)S(1)}, f32[2048]{0:T(1024)}, u32[]{:S(2)}) copy-start(f32[2048]{0:T(1024)} %param.7) | copy-start | bytes 24580
  173.8 55.3 %all-to-all-start.1 = ((bf16[2,1024,1,384]{3,0,2,1:T(2,128)(2,1)}), bf16[2,1024,1,384]{3,0,2,1:T(2,128)(2,1)S(1)}, u32[]{:S(2)}, u32[]{:S(2)}) async-start(bf16[2,1024,1,384]{3,0,2,1:T(2,128)(2,1)} %copy.60), calls=%async_computation.1 | async-start | bytes 3145728 | tf_op jit(solution)/shard_map/all_to_all | solution.py:81
  243.9 15.0 %all-to-all-start.4 = ((f32[16,1,128]{2,1,0:T(1,128)}), f32[16,1,128]{2,1,0:T(1,128)S(1)}, u32[]{:S(2)}, u32[]{:S(2)}) async-start(f32[16,1,128]{2,1,0:T(1,128)} %reshape.111), calls=%async_computation.4 | async-start | bytes 16384 | tf_op jit(solution)/shard_map/all_to_all | solution.py:58
  258.9 12.2 %all-to-all-start.2 = ((f32[16,1,128]{2,1,0:T(1,128)}), f32[16,1,128]{2,1,0:T(1,128)S(1)}, u32[]{:S(2)}, u32[]{:S(2)}) async-start(f32[16,1,128]{2,1,0:T(1,128)} %reshape.113), calls=%async_computation.2 | async-start | bytes 16384 | tf_op jit(solution)/shard_map/all_to_all | solution.py:57
  271.1 24.8 %all-to-all-start.3 = ((f32[32,64,1,128]{3,1,2,0:T(8,128)}), f32[32,64,1,128]{3,1,2,0:T(8,128)}, u32[]{:S(2)}, u32[]{:S(2)}) async-start(f32[32,64,1,128]{3,1,2,0:T(8,128)} %copy.71), calls=%async_computation.3 | async-start | bytes 2097152 | tf_op jit(solution)/shard_map/all_to_all | solution.py:56
  275.5 103.4 %all-gather.5.cloned.1.call-start = ((), (), s32[]{:S(2)}) async-start(), calls=%async_computation.6 | async-start | bytes 8912896 | tf_op jit(solution)/shard_map/all_gather | solution.py:93
  276.4 1.9 copy-start
  283.6 1.9 copy-start
  290.1 10.0 %copy-start.2 = (bf16[128,128]{1,0:T(8,128)(2,1)S(1)}, bf16[128,128]{1,0:T(8,128)(2,1)}, u32[]{:S(2)}) copy-start(bf16[128,128]{1,0:T(8,128)(2,1)} %param.9) | copy-start | bytes 98308
  290.1 88.8 %copy-start.1 = (bf16[2048,128]{1,0:T(8,128)(2,1)S(1)}, bf16[2048,128]{1,0:T(8,128)(2,1)}, u32[]{:S(2)}) copy-start(bf16[2048,128]{1,0:T(8,128)(2,1)} %param.6) | copy-start | bytes 1572868
Sparse Core Ops, SparseCore 0:
  23.0 62.0 all-gather.2
  300.2 78.6 all-gather.4
